TPU v7x, 32 devices: a whole 2x2x4 slice. The times are simulated.
32 devices in a mesh: dp: 8 (over z, x), rep: 4 (over y, core).
Axes of the slice: x: 2, y: 2, z: 4, core: 2. Of those that a mesh axis runs over, the one named last changes fastest.
Arguments:
- hot_ids: int32 [8192, 2], P(('dp', 'rep')), may hold values from 0 to 1023
- cold_owner: int32 [16384, 1], P(('dp', 'rep')), may hold values from 0 to 7; in each aligned block of 512 rows (0 to 511, 512 to 1023, ...) at most 128 rows name the same one
- cold_offset: int32 [16384], P(('dp', 'rep')), may hold values from 0 to 511
- labels: int32 [8192], P(('dp', 'rep')), may hold values 0 or 1
- top_weight: bfloat16 [512, 1024], replicated, may hold values from -0.25 to 0.25
- out_weight: float32 [1024], replicated, may hold values from -0.5 to 0.5
- cold_table: float32 [4096, 128], P('dp'), may hold values from -6 to 6
- cold_accum: float32 [4096, 128], P('dp'), may hold values from 0.0001 to 0.01
- hot_cache: float32 [1024, 128], replicated, may hold values from -6 to 6
- hot_accum: float32 [1024, 128], replicated, may hold values from 0.01 to 1
- pending: float32 [32768, 128], P(('dp', 'rep')), may hold values from -0.3 to 0.3
- refresh_blocks: int32 [3], replicated, may hold values from 0 to 7, as said below
- block_clock: int32 [8], replicated, may hold values from 0 to 8
Outputs:
- cold_table_new: float32 [4096, 128], P('dp')
- cold_accum_new: float32 [4096, 128], P('dp')
- hot_cache_new: float32 [1024, 128], replicated
- hot_accum_new: float32 [1024, 128], replicated
- pending_new: float32 [32768, 128], P(('dp', 'rep'))
- top_grad: float32 [512, 1024], P(('dp', 'rep'))
- out_grad: float32 [1024], replicated
Inputs may be any that keep to these rules, and one draw needn't show every extreme that they name: `cold_owner`: within the lookups of one device (512 rows), no owner is named more than 128 times. `refresh_blocks`: the block numbers are distinct.
All inputs are finite; a program needn't handle non-finite values. No bound on the sum of `labels` on one device may be relied on, other than what follows from the above.
Results may differ from a plain program's by a relative error of at most 0.00165.
The roundings to bfloat16 on the way count: a program that leaves them out, or rounds other values in their place, can miss the bound.
Values may be sent and summed in bfloat16 or wider, within the bound.
A program may use at most 64 MiB of HBM per device.

v0:
```python
import jax
import jax.numpy as jnp
from jax import lax
from jax.sharding import PartitionSpec as P

BLOCK = 128
step_size = 0.5
epsilon = 1e-08


def adagrad(table_rows, accum_rows, gradient):
    accum_next = accum_rows + gradient * gradient
    return (table_rows - step_size * gradient / (jnp.sqrt(accum_next) + epsilon), accum_next)


def local(
    hot_ids,
    cold_owner,
    cold_offset,
    labels,
    top_weight,
    out_weight,
    cold_table,
    cold_accum,
    hot_cache,
    hot_accum,
    pending,
    refresh_blocks,
    block_clock,
):
    width = hot_cache.shape[1]
    samples = hot_ids.shape[0]
    hot_feats = hot_ids.shape[1]
    lookups = cold_offset.shape[0]
    cold_feats = lookups // samples
    owners_count = lax.axis_size("dp")
    capacity = max(2, 2 * lookups // owners_count)
    owners = cold_owner[:, 0]
    matches = (owners[:, None] == jnp.arange(owners_count, dtype=jnp.int32)[None, :]).astype(
        jnp.int32
    )
    earlier = jnp.cumsum(matches, axis=0) - matches
    positions = jnp.sum(earlier * matches, axis=1)
    targets = owners * capacity + positions
    requests = jnp.zeros((owners_count * capacity,), jnp.int32).at[targets].set(cold_offset)
    requests = requests.reshape(owners_count, capacity)
    asked = lax.all_to_all(requests, "dp", split_axis=0, concat_axis=0, tiled=True)
    found = cold_table[asked].astype(jnp.bfloat16)
    returned = lax.all_to_all(found, "dp", split_axis=0, concat_axis=0, tiled=True)
    cold_rows = returned.reshape(owners_count * capacity, width)[targets]
    cold_rows = cold_rows.reshape(samples, cold_feats, width)
    hot_rows = hot_cache[hot_ids].astype(jnp.bfloat16)
    inputs = jnp.concatenate([hot_rows, cold_rows], axis=1).reshape(
        samples, (hot_feats + cold_feats) * width
    )
    preact = jnp.dot(inputs, top_weight, preferred_element_type=jnp.float32)
    hidden = jax.nn.silu(preact).astype(jnp.bfloat16)
    hidden_wide = hidden.astype(jnp.float32)
    logits = jnp.dot(hidden_wide, out_weight, precision=lax.Precision.HIGHEST)
    errors = jax.nn.sigmoid(logits) - labels.astype(jnp.float32)
    gates = jax.nn.sigmoid(preact)
    slope = gates * (1.0 + preact * (1.0 - gates))
    dhidden = (errors[:, None] * out_weight[None, :] * slope).astype(jnp.bfloat16)
    head_term = jnp.dot(errors, hidden_wide, precision=lax.Precision.HIGHEST)
    top_grad = lax.psum_scatter(
        lax.dot_general(
            inputs, dhidden, (((0,), (0,)), ((), ())), preferred_element_type=jnp.float32
        ),
        ("dp", "rep"),
        scatter_dimension=0,
        tiled=True,
    )
    dinputs = lax.dot_general(
        dhidden, top_weight, (((1,), (1,)), ((), ())), preferred_element_type=jnp.float32
    ).astype(jnp.bfloat16)
    dinputs = dinputs.reshape(samples, hot_feats + cold_feats, width)
    cold_dx = dinputs[:, hot_feats:].reshape(lookups, width)
    outgoing = jnp.zeros((owners_count * capacity, width), jnp.bfloat16).at[targets].set(cold_dx)
    outgoing = outgoing.reshape(owners_count, capacity, width)
    incoming = lax.all_to_all(outgoing, "dp", split_axis=0, concat_axis=0, tiled=True)
    own_rows = cold_table.shape[0]
    cold_grad = (
        jnp.zeros((own_rows, width), jnp.float32)
        .at[asked.reshape(-1)]
        .add(incoming.reshape(-1, width).astype(jnp.float32))
    )
    quarter = own_rows // lax.axis_size("rep")
    offset_rows = lax.axis_index("rep") * quarter
    cold_share = lax.psum_scatter(cold_grad, "rep", scatter_dimension=0, tiled=True)
    table_share = lax.dynamic_slice_in_dim(cold_table, offset_rows, quarter, 0)
    accum_share = lax.dynamic_slice_in_dim(cold_accum, offset_rows, quarter, 0)
    table_updated, accum_updated = adagrad(table_share, accum_share, cold_share)
    cold_table_new, cold_accum_new = (
        lax.all_gather(table_updated, "rep", axis=0, tiled=True),
        lax.all_gather(accum_updated, "rep", axis=0, tiled=True),
    )
    hot_count = hot_cache.shape[0]
    blocks_count = hot_count // BLOCK
    hot_dx = dinputs[:, :hot_feats].reshape(samples * hot_feats, width).astype(jnp.float32)
    hot_grad = jnp.zeros((hot_count, width), jnp.float32).at[hot_ids.reshape(-1)].add(hot_dx)
    carried = (pending + hot_grad).reshape(blocks_count, BLOCK, width)
    picked = carried[refresh_blocks]
    divisors = 1.0 + block_clock[refresh_blocks].astype(jnp.float32)
    cache_blocks = hot_cache.reshape(blocks_count, BLOCK, width)
    accum_blocks = hot_accum.reshape(blocks_count, BLOCK, width)
    cache_chosen = cache_blocks[refresh_blocks]
    accum_chosen = accum_blocks[refresh_blocks]
    picked_sum, out_grad = lax.psum((picked, head_term), ("dp", "rep"))
    flush = picked_sum / divisors[:, None, None]
    cache_part, accum_part = adagrad(cache_chosen, accum_chosen, flush)
    hot_cache_new = cache_blocks.at[refresh_blocks].set(cache_part).reshape(hot_count, width)
    hot_accum_new = accum_blocks.at[refresh_blocks].set(accum_part).reshape(hot_count, width)
    pending_new = carried.at[refresh_blocks].set(0.0).reshape(hot_count, width)
    return (
        cold_table_new,
        cold_accum_new,
        hot_cache_new,
        hot_accum_new,
        pending_new,
        top_grad,
        out_grad,
    )


def solution(mesh):
    in_specs = (
        P(("dp", "rep"), None),
        P(("dp", "rep"), None),
        P(("dp", "rep")),
        P(("dp", "rep")),
        P(),
        P(),
        P("dp", None),
        P("dp", None),
        P(),
        P(),
        P(("dp", "rep"), None),
        P(),
        P(),
    )
    out_specs = (
        P("dp", None),
        P("dp", None),
        P(),
        P(),
        P(("dp", "rep"), None),
        P(("dp", "rep"), None),
        P(),
    )
    return jax.shard_map(local, mesh=mesh, in_specs=in_specs, out_specs=out_specs, check_vma=False)
```

profile of v0, /device:TPU:0, one launch (start us, length us, event | category | flops | bytes accessed | tf_op | source)
XLA Modules:
  0.0 244.3 jit_solution(7436814418134962637)
XLA Ops:
  8.0 1.2 copy.44
  9.4 1.1 reduce-window.6
  10.9 2.6 %scatter_custom_fusion = s32[1024]{0:T(1024)S(1)} fusion(s32[512]{0:T(512)S(1)} %bitcast.83, s32[512]{0:T(512)} %param.15, s32[]{:T(128)} %constant.13.clone.1), kind=kCustom, calls=%fused_computation.55 | custom fusion | bytes 4608 | tf_op jit(solution)/shard_map/scatter | solution.py:45
  13.5 13.6 %all_to_all.22 = s32[8,1,128]{2,1,0:T(1,128)S(1)} all-to-all(s32[8,1,128]{2,1,0:T(1,128)S(1)} %bitcast.82), channel_id=1, replica_groups=mesh['dp'=8,'rep'=4] {'dp'}, dimensions={0} | all-to-all | bytes 8192 | tf_op jit(solution)/shard_map/all_to_all | solution.py:47
  27.1 4.1 %gather_fusion.1 = bf16[1024,128]{1,0:T(8,128)(2,1)} fusion(f32[512,128]{1,0:T(8,128)S(1)} %copy-done.2, s32[1024]{0:T(1024)S(1)} %fusion.17), kind=kCustom, calls=%fused_computation.1 | custom fusion | bytes 528384 | tf_op jit(solution)/shard_map/gather | solution.py:48
  31.2 3.4 %all-to-all-start.1 = ((bf16[8,128,128]{2,1,0:T(8,128)(2,1)}), bf16[8,128,128]{2,1,0:T(8,128)(2,1)S(1)}, u32[]{:S(2)}, u32[]{:S(2)}) async-start(bf16[8,128,128]{2,1,0:T(8,128)(2,1)} %bitcast.12), calls=%async_computation.1 | async-start | bytes 524288 | tf_op jit(solution)/shard_map/all_to_all | solution.py:49
  35.0 1.1 gather_fusion
  36.6 6.2 %all-to-all-done.1 = bf16[8,128,128]{2,1,0:T(8,128)(2,1)S(1)} async-done(((bf16[8,128,128]{2,1,0:T(8,128)(2,1)}), bf16[8,128,128]{2,1,0:T(8,128)(2,1)S(1)}, u32[]{:S(2)}, u32[]{:S(2)}) %all-to-all-start.1) | async-done | bytes 262176 | tf_op jit(solution)/shard_map/all_to_all | solution.py:49
  42.8 1.3 gather_fusion.2
  46.3 1.3 convolution_convert_fusion
  47.6 1.8 reshape.179
  49.4 1.9 fusion.20
  51.3 2.8 %scatter_custom_fusion.1 = bf16[1024,128]{1,0:T(8,128)(2,1)} fusion(s32[512]{0:T(512)S(1)} %bitcast.85, bf16[512,128]{1,0:T(8,128)(2,1)} %bitcast.77, bf16[]{:T(256)} %constant.17.clone.1), kind=kCustom, calls=%fused_computation.31 | custom fusion | bytes 262656 | tf_op jit(solution)/shard_map/scatter | solution.py:78
  54.1 4.0 %all-to-all-start.2 = ((bf16[8,128,128]{2,1,0:T(8,128)(2,1)}), bf16[8,128,128]{2,1,0:T(8,128)(2,1)}, u32[]{:S(2)}, u32[]{:S(2)}) async-start(bf16[8,128,128]{2,1,0:T(8,128)(2,1)} %bitcast.71), calls=%async_computation.2 | async-start | bytes 524288 | tf_op jit(solution)/shard_map/all_to_all | solution.py:80
  58.2 0.8 copy.22
  59.0 1.1 reshape.183
  60.6 3.6 %scatter_custom_fusion.3 = f32[1024,128]{1,0:T(8,128)S(1)} fusion(f32[1024,128]{1,0:T(8,128)S(1)} %copy-done.6, s32[512]{0:T(512)} %bitcast.91, bf16[512,128]{1,0:T(8,128)(2,1)S(1)} %bitcast.72), kind=kCustom, calls=%fused_computation.25 | custom fusion | flops 131072 | bytes 655360 | tf_op jit(solution)/shard_map/scatter-add | solution.py:100
  64.3 1.2 gather_fusion.4
  65.6 0.7 all-to-all-done.2
  66.3 7.1 %scatter_custom_fusion.2 = f32[512,128]{1,0:T(8,128)} fusion(s32[1024]{0:T(1024)S(1)} %bitcast.90, bf16[1024,128]{1,0:T(8,128)(2,1)} %bitcast.31, f32[]{:T(128)} %constant.15.clone.1), kind=kCustom, calls=%fused_computation.18 | custom fusion | flops 262144 | bytes 524292 | tf_op jit(solution)/shard_map/scatter-add | solution.py:85
  73.7 3.4 %fusion.2 = f32[512,1024]{1,0:T(8,128)} fusion(bf16[32,8,4,128]{3,2,1,0:T(4,128)(2,1)} %bitcast.76, f32[256,1024]{1,0:T(8,128)} %copy-done.18, f32[1024]{0:T(1024)} %param.18, f32[256]{0:T(256)S(1)} %copy-done.15), kind=kOutput, calls=%fused_computation.20 | convolution fusion | flops 271056896 | bytes 3412992 | tf_op jit(solution)/shard_map/dot_general | solution.py:66
  78.3 1.2 gather_fusion.3
  79.6 1.2 gather_fusion.6
  81.5 1.5 scatter_fusion.2
  83.4 41.0 %psum.15 = f32[1024]{0:T(1024)} all-reduce(f32[1024]{0:T(1024)S(1)} %bitcast.81), channel_id=1, replica_groups=mesh['dp'=8,'rep'=4] {'dp','rep'}, use_global_device_ids=true, to_apply=%region_13.14 | all-reduce | flops 1024 | bytes 8192 | tf_op jit(solution)/shard_map/psum | solution.py:108
  124.4 67.7 %all-reduce.2.cloned.1.call-done = f32[3,128,128]{2,1,0:T(8,128)} async-done(((f32[3,128,128]{2,1,0:T(8,128)}), f32[3,128,128]{2,1,0:T(8,128)}) %all-reduce.2.cloned.1.call-update) | async-done | bytes 196624 | tf_op jit(solution)/shard_map/psum | solution.py:108
  192.1 1.3 multiply_add_fusion
  194.8 1.1 multiply_add_fusion.1
  195.8 6.4 %all_gather.7 = f32[512,128]{1,0:T(8,128)S(1)} all-gather(f32[128,128]{1,0:T(8,128)S(1)} %get-tuple-element.9), channel_id=1, replica_groups=mesh['dp'=8,'rep'=4] {'rep'}, dimensions={0}, use_global_device_ids=true | all-gather | bytes 327680 | tf_op jit(solution)/shard_map/all_gather | solution.py:95
  202.2 6.1 %all_gather.6 = f32[512,128]{1,0:T(8,128)S(1)} all-gather(f32[128,128]{1,0:T(8,128)S(1)} %get-tuple-element.10), channel_id=1, replica_groups=mesh['dp'=8,'rep'=4] {'rep'}, dimensions={0}, use_global_device_ids=true | all-gather | bytes 327680 | tf_op jit(solution)/shard_map/all_gather | solution.py:94
  208.3 27.2 %reduce-scatter.5.cloned.1.call-done = f32[16,1024]{1,0:T(8,128)} async-done(((f32[512,1024]{1,0:T(8,128)}), f32[16,1024]{1,0:T(8,128)}) %reduce-scatter.5.cloned.1.call-update) | async-done | bytes 65552 | tf_op jit(solution)/shard_map/reduce_scatter | solution.py:65
  236.2 0.7 copy.48
  (73 shorter events, 8.7 us)
Async XLA Ops:
  8.0 36.4 %copy-start = (bf16[512,1024]{1,0:T(8,128)(2,1)S(1)}, bf16[512,1024]{1,0:T(8,128)(2,1)}, u32[]{:S(2)}) copy-start(bf16[512,1024]{1,0:T(8,128)(2,1)} %param.17) | copy-start | bytes 3145732
  8.0 1.4 copy-start.9
  8.0 19.1 %copy-start.2 = (f32[512,128]{1,0:T(8,128)S(1)}, f32[512,128]{1,0:T(8,128)}, u32[]{:S(2)}) copy-start(f32[512,128]{1,0:T(8,128)} %param.19) | copy-start | bytes 786436
  8.0 1.3 copy-start.7
  9.3 25.3 %copy-start.10 = (s32[256,2]{0,1:T(2,128)S(1)}, s32[256,2]{0,1:T(2,128)}, u32[]{:S(2)}) copy-start(s32[256,2]{0,1:T(2,128)} %param.13) | copy-start | bytes 6148
  27.1 8.9 %copy-start.17 = (s32[3]{0:T(128)S(1)}, s32[3]{0:T(128)}, u32[]{:S(2)}) copy-start(s32[3]{0:T(128)} %param.24) | copy-start | bytes 40
  31.2 11.6 %all-to-all-start.1 = ((bf16[8,128,128]{2,1,0:T(8,128)(2,1)}), bf16[8,128,128]{2,1,0:T(8,128)(2,1)S(1)}, u32[]{:S(2)}, u32[]{:S(2)}) async-start(bf16[8,128,128]{2,1,0:T(8,128)(2,1)} %bitcast.12), calls=%async_computation.1 | async-start | bytes 524288 | tf_op jit(solution)/shard_map/all_to_all | solution.py:49
  44.4 0.7 copy-start.8
  44.4 0.7 copy-start.13
  44.4 1.2 copy-start.16
  45.1 1.0 copy-start.18
  45.7 0.6 copy-start.14
  46.3 11.9 %copy-start.11 = (s32[3]{0:T(128)S(1)}, s32[3]{0:T(128)}, u32[]{:S(2)}) copy-start(s32[3]{0:T(128)} %compare_select_fusion.5) | copy-start | bytes 40
  47.6 13.0 %copy-start.6 = (f32[1024,128]{1,0:T(8,128)S(1)}, f32[1024,128]{1,0:T(8,128)}, u32[]{:S(2)}) copy-start(f32[1024,128]{1,0:T(8,128)} %param.23) | copy-start | bytes 1572868
  54.1 12.3 %all-to-all-start.2 = ((bf16[8,128,128]{2,1,0:T(8,128)(2,1)}), bf16[8,128,128]{2,1,0:T(8,128)(2,1)}, u32[]{:S(2)}, u32[]{:S(2)}) async-start(bf16[8,128,128]{2,1,0:T(8,128)(2,1)} %bitcast.71), calls=%async_computation.2 | async-start | bytes 524288 | tf_op jit(solution)/shard_map/all_to_all | solution.py:80
  58.1 134.0 %all-reduce.2.cloned.1.call-start = ((), (), s32[]{:S(2)}) async-start(), calls=%async_computation.6 | async-start | bytes 393216 | tf_op jit(solution)/shard_map/psum | solution.py:108
  59.0 14.7 %copy-start.15 = (f32[256]{0:T(256)S(1)}, f32[256]{0:T(256)}, u32[]{:S(2)}) copy-start(f32[256]{0:T(256)} %copy-done.14) | copy-start | bytes 3076
  65.5 129.2 %reduce-scatter.3.cloned.1.call-start = ((), (), s32[]{:S(2)}) async-start(), calls=%async_computation.5 | async-start | bytes 327680 | tf_op jit(solution)/shard_map/reduce_scatter | solution.py:89
  73.4 162.1 %reduce-scatter.5.cloned.1.call-start = ((), (), s32[]{:S(2)}) async-start(), calls=%async_computation.7 | async-start | bytes 2162688 | tf_op jit(solution)/shard_map/reduce_scatter | solution.py:65
  77.0 0.7 copy-start.1
  77.1 4.5 %copy-start.12 = (s32[3]{0:T(128)S(1)}, s32[3]{0:T(128)}, u32[]{:S(2)}) copy-start(s32[3]{0:T(128)} %compare_select_fusion.5) | copy-start | bytes 40
  83.1 153.1 %copy-start.5 = (f32[8,128,128]{2,1,0:T(8,128)}, f32[8,128,128]{2,1,0:T(8,128)S(1)}, u32[]{:S(2)}) copy-start(f32[8,128,128]{2,1,0:T(8,128)S(1)} %scatter_fusion.2) | copy-start | bytes 1572868
  194.0 42.9 %copy-start.4 = (f32[8,128,128]{2,1,0:T(8,128)}, f32[8,128,128]{2,1,0:T(8,128)S(1)}, u32[]{:S(2)}) copy-start(f32[8,128,128]{2,1,0:T(8,128)S(1)} %scatter_fusion.1) | copy-start | bytes 1572868
  194.7 42.2 %copy-start.3 = (f32[8,128,128]{2,1,0:T(8,128)}, f32[8,128,128]{2,1,0:T(8,128)S(1)}, u32[]{:S(2)}) copy-start(f32[8,128,128]{2,1,0:T(8,128)S(1)} %scatter_fusion) | copy-start | bytes 1572868
Sparse Core Ops, SparseCore 0:
  65.7 126.3 all-reduce.1
Sparse Core Ops, SparseCore 1:
  73.5 21.1 reduce-scatter.2
  97.3 138.1 reduce-scatter.4
where the time goes:
time: 245 us; the launch traced here: 244 us
  waiting for transfers between devices  102 us (42%)
  blocking collectives  67 us (27%)
  local copies, waits for them, and re-layouts  30 us (12%)
  other arithmetic  15.8 us (6%)
  between operations  15.8 us (6%)
  starting transfers between devices  7.76 us (3%)
  matrix products  6.01 us (2%)
    psum x1, waiting for transfers between devices, local(): picked_sum, out_grad = lax.psum((picked, head_term), ('dp', 'rep'))  67.7 us
    psum x1, blocking collectives, local(): picked_sum, out_grad = lax.psum((picked, head_term), ('dp', 'rep'))  41 us
    reduce_scatter x1, waiting for transfers between devices, local(): lax.psum_scatter(lax.dot_general(inputs, dhidden, (((0,), (0,)), ((), ())...  27.2 us
    all_to_all x1, blocking collectives, local(): lax.all_to_all(requests, 'dp', split_axis=0, concat_axis=0, tiled=True)  13.6 us
    scatter-add x1, other arithmetic, local(): cold_grad = jnp.zeros((own_rows, width), jnp.float32).at[asked.reshape(-1...  7.07 us
    all_gather x1, blocking collectives, local(): lax.all_gather(accum_updated, 'rep', axis=0, tiled=True)  6.39 us
    all_to_all x1, waiting for transfers between devices, local(): lax.all_to_all(found, 'dp', split_axis=0, concat_axis=0, tiled=True)  6.23 us
    all_gather x1, blocking collectives, local(): lax.all_gather(table_updated, 'rep', axis=0, tiled=True)  6.1 us
  transfers between devices with their start and end apart: 5, of which 4 were waited for; matrix products, arithmetic and copies ran while one was open for 12% of the time, Pallas kernels for 0%

commit v1 on v0

--- a/solution.py
+++ b/solution.py
@@ -2,10 +2,17 @@
 import jax.numpy as jnp
 from jax import lax
 from jax.sharding import PartitionSpec as P
+from jax.lax import psum
 
 BLOCK = 128
 step_size = 0.5
 epsilon = 1e-08
+
+
+def define_layers_all(s0):
+    for hop_no in ("rep", "dp"):
+        s0 = psum(s0, hop_no)
+    return s0
 
 
 def adagrad(table_rows, accum_rows, gradient):
@@ -105,7 +112,7 @@
     accum_blocks = hot_accum.reshape(blocks_count, BLOCK, width)
     cache_chosen = cache_blocks[refresh_blocks]
     accum_chosen = accum_blocks[refresh_blocks]
-    picked_sum, out_grad = lax.psum((picked, head_term), ("dp", "rep"))
+    picked_sum, out_grad = define_layers_all((picked, head_term))
     flush = picked_sum / divisors[:, None, None]
     cache_part, accum_part = adagrad(cache_chosen, accum_chosen, flush)
     hot_cache_new = cache_blocks.at[refresh_blocks].set(cache_part).reshape(hot_count, width)

time: 245 us -> 342 us (1.40)
  waiting for transfers between devices: 102 us -> 216 us
  blocking collectives: 67 us -> 53.5 us
    reduce_scatter x1, waiting for transfers between devices: 27.2 us -> 128 us  [local(): lax.psum_scatter(lax.dot_general(inputs, dhidden, (((0,), (0,)), ((), ())...]
    reduce_scatter x1, waiting for transfers between devices: 0.03 us -> 19.5 us  [local(): lax.psum_scatter(cold_grad, 'rep', scatter_dimension=0, tiled=True)]
    psum x1 -> x2, blocking collectives: 41 us -> 28 us  [define_layers_all(): s0 = psum(s0, hop_no)]
    psum x1 -> x2, waiting for transfers between devices: 67.7 us -> 62.3 us  [define_layers_all(): s0 = psum(s0, hop_no)]
  transfers between devices with their start and end apart: 5 -> 6, of which waited for: 4 -> 5; matrix products, arithmetic and copies ran while one was open for 12% -> 8% of each run, Pallas kernels for 0% -> 0%
where the time goes in v1:
time: 342 us; the launch traced here: 341 us
  waiting for transfers between devices  216 us (63%)
  blocking collectives  53.5 us (16%)
  local copies, waits for them, and re-layouts  28.2 us (8%)
  other arithmetic  15.8 us (5%)
  between operations  14.1 us (4%)
  starting transfers between devices  7.8 us (2%)
  matrix products  6.01 us (2%)
    reduce_scatter x1, waiting for transfers between devices, local(): lax.psum_scatter(lax.dot_general(inputs, dhidden, (((0,), (0,)), ((), ())...  128 us
    psum x2, waiting for transfers between devices, define_layers_all(): s0 = psum(s0, hop_no)  62.3 us
    psum x2, blocking collectives, define_layers_all(): s0 = psum(s0, hop_no)  28 us
    reduce_scatter x1, waiting for transfers between devices, local(): lax.psum_scatter(cold_grad, 'rep', scatter_dimension=0, tiled=True)  19.5 us
    all_to_all x1, blocking collectives, local(): lax.all_to_all(requests, 'dp', split_axis=0, concat_axis=0, tiled=True)  13.6 us
    scatter-add x1, other arithmetic, local(): cold_grad = jnp.zeros((own_rows, width), jnp.float32).at[asked.reshape(-1...  7.08 us
  transfers between devices with their start and end apart: 6, of which 5 were waited for; matrix products, arithmetic and copies ran while one was open for 8% of the time, Pallas kernels for 0%

profile of v1, /device:TPU:0, one launch (start us, length us, event | category | flops | bytes accessed | tf_op | source)
XLA Modules:
  0.0 341.0 jit_solution(10984362844100420754)
XLA Ops:
  7.2 1.2 copy.45
  8.6 1.1 reduce-window.6
  10.1 2.6 scatter_custom_fusion
  12.7 13.6 %all_to_all.22 = s32[8,1,128]{2,1,0:T(1,128)S(1)} all-to-all(s32[8,1,128]{2,1,0:T(1,128)S(1)} %bitcast.82), channel_id=1, replica_groups=mesh['dp'=8,'rep'=4] {'dp'}, dimensions={0} | all-to-all | bytes 8192 | tf_op jit(solution)/shard_map/all_to_all | solution.py:54
  26.3 4.1 %gather_fusion.1 = bf16[1024,128]{1,0:T(8,128)(2,1)} fusion(f32[512,128]{1,0:T(8,128)S(1)} %copy-done.2, s32[1024]{0:T(1024)S(1)} %fusion.17), kind=kCustom, calls=%fused_computation.1 | custom fusion | bytes 528384 | tf_op jit(solution)/shard_map/gather | solution.py:55
  30.4 3.4 %all-to-all-start.1 = ((bf16[8,128,128]{2,1,0:T(8,128)(2,1)}), bf16[8,128,128]{2,1,0:T(8,128)(2,1)S(1)}, u32[]{:S(2)}, u32[]{:S(2)}) async-start(bf16[8,128,128]{2,1,0:T(8,128)(2,1)} %bitcast.12), calls=%async_computation.1 | async-start | bytes 524288 | tf_op jit(solution)/shard_map/all_to_all | solution.py:56
  34.4 1.1 gather_fusion
  36.1 5.9 %all-to-all-done.1 = bf16[8,128,128]{2,1,0:T(8,128)(2,1)S(1)} async-done(((bf16[8,128,128]{2,1,0:T(8,128)(2,1)}), bf16[8,128,128]{2,1,0:T(8,128)(2,1)S(1)}, u32[]{:S(2)}, u32[]{:S(2)}) %all-to-all-start.1) | async-done | bytes 262176 | tf_op jit(solution)/shard_map/all_to_all | solution.py:56
  41.9 1.3 gather_fusion.2
  45.3 1.3 convolution_convert_fusion
  46.6 1.7 reshape.179
  48.3 1.9 fusion.20
  50.2 2.8 scatter_custom_fusion.1
  53.0 4.0 %all-to-all-start.2 = ((bf16[8,128,128]{2,1,0:T(8,128)(2,1)}), bf16[8,128,128]{2,1,0:T(8,128)(2,1)}, u32[]{:S(2)}, u32[]{:S(2)}) async-start(bf16[8,128,128]{2,1,0:T(8,128)(2,1)} %bitcast.71), calls=%async_computation.2 | async-start | bytes 524288 | tf_op jit(solution)/shard_map/all_to_all | solution.py:87
  57.8 3.7 %scatter_custom_fusion.3 = f32[1024,128]{1,0:T(8,128)S(1)} fusion(f32[1024,128]{1,0:T(8,128)S(1)} %copy-done.6, s32[512]{0:T(512)} %bitcast.91, bf16[512,128]{1,0:T(8,128)(2,1)S(1)} %bitcast.72), kind=kCustom, calls=%fused_computation.25 | custom fusion | flops 131072 | bytes 655360 | tf_op jit(solution)/shard_map/scatter-add | solution.py:107
  61.4 1.2 gather_fusion.4
  62.7 33.4 %all-reduce.3.cloned.1.call-done = f32[3,128,128]{2,1,0:T(8,128)} async-done(((f32[3,128,128]{2,1,0:T(8,128)}), f32[3,128,128]{2,1,0:T(8,128)}) %all-reduce.3.cloned.1.call-update) | async-done | bytes 196624 | tf_op jit(solution)/shard_map/psum | solution.py:14
  96.2 7.1 %scatter_custom_fusion.2 = f32[512,128]{1,0:T(8,128)} fusion(s32[1024]{0:T(1024)S(1)} %bitcast.90, bf16[1024,128]{1,0:T(8,128)(2,1)} %bitcast.31, f32[]{:T(128)} %constant.15.clone.1), kind=kCustom, calls=%fused_computation.18 | custom fusion | flops 262144 | bytes 524292 | tf_op jit(solution)/shard_map/scatter-add | solution.py:92
  103.6 3.4 fusion.2
  108.2 1.2 gather_fusion.3
  109.5 1.2 gather_fusion.6
  111.4 1.5 scatter_fusion.2
  113.3 5.7 %psum.30 = f32[1024]{0:T(1024)S(1)} all-reduce(f32[1024]{0:T(1024)S(1)} %bitcast.81), channel_id=1, replica_groups=mesh['dp'=8,'rep'=4] {'rep'}, use_global_device_ids=true, to_apply=%region_14.15 | all-reduce | flops 1024 | bytes 8192 | tf_op jit(solution)/shard_map/psum | solution.py:14
  119.0 22.2 %psum.31 = f32[1024]{0:T(1024)} all-reduce(f32[1024]{0:T(1024)S(1)} %psum.30), channel_id=1, replica_groups=mesh['dp'=8,'rep'=4] {'dp'}, use_global_device_ids=true, to_apply=%region_15.16 | all-reduce | flops 1024 | bytes 8192 | tf_op jit(solution)/shard_map/psum | solution.py:14
  141.2 28.9 %all-reduce.5.cloned.1.call-done = f32[3,128,128]{2,1,0:T(8,128)} async-done(((f32[3,128,128]{2,1,0:T(8,128)}), f32[3,128,128]{2,1,0:T(8,128)}) %all-reduce.5.cloned.1.call-update) | async-done | bytes 196624 | tf_op jit(solution)/shard_map/psum | solution.py:14
  170.2 1.3 multiply_add_fusion
  172.8 19.5 %reduce-scatter.3.cloned.1.call-done = f32[128,128]{1,0:T(8,128)} async-done(((f32[512,128]{1,0:T(8,128)}), f32[128,128]{1,0:T(8,128)}) %reduce-scatter.3.cloned.1.call-update) | async-done | bytes 65552 | tf_op jit(solution)/shard_map/reduce_scatter | solution.py:96
  192.3 0.9 multiply_add_fusion.1
  193.3 5.8 %all_gather.7 = f32[512,128]{1,0:T(8,128)S(1)} all-gather(f32[128,128]{1,0:T(8,128)S(1)} %get-tuple-element.9), channel_id=1, replica_groups=mesh['dp'=8,'rep'=4] {'rep'}, dimensions={0}, use_global_device_ids=true | all-gather | bytes 327680 | tf_op jit(solution)/shard_map/all_gather | solution.py:102
  199.0 6.2 %all_gather.6 = f32[512,128]{1,0:T(8,128)S(1)} all-gather(f32[128,128]{1,0:T(8,128)S(1)} %get-tuple-element.10), channel_id=1, replica_groups=mesh['dp'=8,'rep'=4] {'rep'}, dimensions={0}, use_global_device_ids=true | all-gather | bytes 327680 | tf_op jit(solution)/shard_map/all_gather | solution.py:101
  205.2 127.8 %reduce-scatter.5.cloned.1.call-done = f32[16,1024]{1,0:T(8,128)} async-done(((f32[512,1024]{1,0:T(8,128)}), f32[16,1024]{1,0:T(8,128)}) %reduce-scatter.5.cloned.1.call-update) | async-done | bytes 65552 | tf_op jit(solution)/shard_map/reduce_scatter | solution.py:72
  333.8 0.7 copy.49
  (71 shorter events, 9.0 us)
Async XLA Ops:
  7.2 36.4 %copy-start = (bf16[512,1024]{1,0:T(8,128)(2,1)S(1)}, bf16[512,1024]{1,0:T(8,128)(2,1)}, u32[]{:S(2)}) copy-start(bf16[512,1024]{1,0:T(8,128)(2,1)} %param.17) | copy-start | bytes 3145732
  7.2 1.4 copy-start.9
  7.2 19.1 %copy-start.2 = (f32[512,128]{1,0:T(8,128)S(1)}, f32[512,128]{1,0:T(8,128)}, u32[]{:S(2)}) copy-start(f32[512,128]{1,0:T(8,128)} %param.19) | copy-start | bytes 786436
  7.2 1.3 copy-start.7
  8.5 25.3 %copy-start.10 = (s32[256,2]{0,1:T(2,128)S(1)}, s32[256,2]{0,1:T(2,128)}, u32[]{:S(2)}) copy-start(s32[256,2]{0,1:T(2,128)} %param.13) | copy-start | bytes 6148
  30.4 11.6 %all-to-all-start.1 = ((bf16[8,128,128]{2,1,0:T(8,128)(2,1)}), bf16[8,128,128]{2,1,0:T(8,128)(2,1)S(1)}, u32[]{:S(2)}, u32[]{:S(2)}) async-start(bf16[8,128,128]{2,1,0:T(8,128)(2,1)} %bitcast.12), calls=%async_computation.1 | async-start | bytes 524288 | tf_op jit(solution)/shard_map/all_to_all | solution.py:56
  43.6 0.7 copy-start.8
  43.6 0.7 copy-start.11
  43.6 1.2 copy-start.14
  44.3 1.0 copy-start.15
  44.9 1.7 copy-start.12
  45.3 12.5 %copy-start.6 = (f32[1024,128]{1,0:T(8,128)S(1)}, f32[1024,128]{1,0:T(8,128)}, u32[]{:S(2)}) copy-start(f32[1024,128]{1,0:T(8,128)} %param.23) | copy-start | bytes 1572868
  53.0 43.2 %all-to-all-start.2 = ((bf16[8,128,128]{2,1,0:T(8,128)(2,1)}), bf16[8,128,128]{2,1,0:T(8,128)(2,1)}, u32[]{:S(2)}, u32[]{:S(2)}) async-start(bf16[8,128,128]{2,1,0:T(8,128)(2,1)} %bitcast.71), calls=%async_computation.2 | async-start | bytes 524288 | tf_op jit(solution)/shard_map/all_to_all | solution.py:87
  57.0 39.1 %all-reduce.3.cloned.1.call-start = ((), (), s32[]{:S(2)}) async-start(), calls=%async_computation.6 | async-start | bytes 393216 | tf_op jit(solution)/shard_map/psum | solution.py:14
  62.7 107.5 %all-reduce.5.cloned.1.call-start = ((), (), s32[]{:S(2)}) async-start(), calls=%async_computation.7 | async-start | bytes 393216 | tf_op jit(solution)/shard_map/psum | solution.py:14
  96.2 96.2 %reduce-scatter.3.cloned.1.call-start = ((), (), s32[]{:S(2)}) async-start(), calls=%async_computation.5 | async-start | bytes 327680 | tf_op jit(solution)/shard_map/reduce_scatter | solution.py:96
  103.3 229.7 %reduce-scatter.5.cloned.1.call-start = ((), (), s32[]{:S(2)}) async-start(), calls=%async_computation.8 | async-start | bytes 2162688 | tf_op jit(solution)/shard_map/reduce_scatter | solution.py:72
  106.9 0.7 copy-start.1
  106.9 6.0 %copy-start.13 = (f32[256]{0:T(256)S(1)}, f32[256]{0:T(256)}, u32[]{:S(2)}) copy-start(f32[256]{0:T(256)} %copy-done.12) | copy-start | bytes 3076
  112.9 220.8 %copy-start.5 = (f32[8,128,128]{2,1,0:T(8,128)}, f32[8,128,128]{2,1,0:T(8,128)S(1)}, u32[]{:S(2)}) copy-start(f32[8,128,128]{2,1,0:T(8,128)S(1)} %scatter_fusion.2) | copy-start | bytes 1572868
  172.1 162.4 %copy-start.4 = (f32[8,128,128]{2,1,0:T(8,128)}, f32[8,128,128]{2,1,0:T(8,128)S(1)}, u32[]{:S(2)}) copy-start(f32[8,128,128]{2,1,0:T(8,128)S(1)} %scatter_fusion.1) | copy-start | bytes 1572868
  172.8 161.7 %copy-start.3 = (f32[8,128,128]{2,1,0:T(8,128)}, f32[8,128,128]{2,1,0:T(8,128)S(1)}, u32[]{:S(2)}) copy-start(f32[8,128,128]{2,1,0:T(8,128)S(1)} %scatter_fusion) | copy-start | bytes 1572868
Sparse Core Ops, SparseCore 0:
  62.8 33.2 all-reduce.2
  99.4 70.6 all-reduce.4
  173.2 19.1 reduce-scatter.2
  195.0 137.9 reduce-scatter.4
